TPU v7x, 512 devices: a whole 4x4x16 slice. The times are simulated.
512 devices in a mesh: row: 16 (over y, x), col: 16 (over z), depth: 2 (over core).
Axes of the slice: x: 4, y: 4, z: 16, core: 2. Of those that a mesh axis runs over, the one named last changes fastest.
Arguments:
- left_store: float32 [16, 2, 16, 2, 64, 1024], P('row', 'depth', 'col'), may hold values from -6 to 6
- left_home: int32 [16, 2, 16], P('row', 'depth'), may hold values from 0 to 15, each once within a row
- up_store: float32 [16, 2, 16, 2, 64, 1024], P('col', 'depth', 'row'), may hold values from -0.3125 to 0.3125
- up_home: int32 [16, 2, 16], P('col', 'depth'), may hold values from 0 to 15, each once within a row
- targets: int32 [16, 16, 2], P('row', 'col'), may hold values from 0 to 63, as said below
- sketch: float32 [16, 16, 2, 64, 1024], P('row', 'col'), may hold values from -0.1875 to 0.1875
Outputs:
- basis: float32 [16, 16, 2, 64, 1024], P('row', 'col', 'depth')
- weights: float32 [16, 16, 2, 64, 1024], P('row', 'col', 'depth')
Inputs may be any that keep to these rules, and one draw needn't show every extreme that they name: `left_home`: for each row and depth index the entries are the store positions 0 to 15, each once. `up_home`: for each col and depth index the entries are the store positions 0 to 15, each once. `targets`: the 2 entries of one row and col index are distinct.
All inputs are finite; a program needn't handle non-finite values.
Results may differ from a plain program's by a relative error of at most 0.0003.
Values sent between devices are 32-bit elements; how exact they have to be, the bound alone decides.
No kernel may reach another device: no remote copies, remote signals or barrier semaphores. Data moves between devices by JAX's collectives and lax.ppermute only.
A program may use at most 128 MiB of HBM per device.

v0:
```python
import math
import jax
import jax.numpy as jnp
from jax import lax
from jax.sharding import PartitionSpec as P

KD = 2
RB = 8
CB = 8


def split_up(shard, dim, devices):
    before, after = (shard.shape[:dim], shard.shape[dim + 1 :])
    return jnp.moveaxis(shard.reshape(*before, devices, -1, *after), dim, 0)


def sent_and_summed(shard, axis, dim):
    devices = lax.axis_size(axis)
    pieces = lax.all_to_all(split_up(shard, dim, devices), axis, 0, 0, tiled=True)
    return jnp.sum(pieces, axis=0)


def laid_out(pieces, dim):
    pieces = jnp.moveaxis(pieces, 0, dim)
    shape = pieces.shape
    return pieces.reshape(*shape[:dim], shape[dim] * shape[dim + 1], *shape[dim + 2 :])


def copy_for_each(shard, axis):
    devices = lax.axis_size(axis)
    return lax.all_to_all(
        jnp.broadcast_to(shard[None], (devices, *shard.shape)), axis, 0, 0, tiled=True
    )


def gathered_copies(shard, axis, dim):
    return laid_out(copy_for_each(shard, axis), dim)


def orthonormal(sample):
    gram_mat = jnp.einsum("pat,pbt->pab", sample, sample, precision=lax.Precision.HIGHEST)
    factor_low = jnp.linalg.cholesky(gram_mat)
    return lax.linalg.triangular_solve(factor_low, sample, left_side=True, lower=True)


def shards(left_store, left_home, up_store, up_home, targets, sketch):
    high = lax.Precision.HIGHEST
    left_local = left_store[0, 0]
    up_local = up_store[0, 0]
    left_table = left_home[0, 0]
    up_table = up_home[0, 0]
    left_all = lax.all_gather(left_local, "col", axis=0, tiled=True)
    up_all = lax.all_gather(up_local, "row", axis=0, tiled=True)
    left_pairs = jnp.take(left_all, left_table, axis=0)
    up_pairs = jnp.take(up_all, up_table, axis=0)
    chosen = targets[0, 0]
    block_row = chosen // CB
    block_col = chosen % CB
    row_pairs = jnp.take(left_pairs.reshape((RB, KD) + left_local.shape[1:]), block_row, axis=0)
    col_pairs = jnp.take(up_pairs.reshape((CB, KD) + up_local.shape[1:]), block_col, axis=0)
    row_basis = row_pairs[:, :, 0]
    row_coef = row_pairs[:, :, 1]
    col_coef = col_pairs[:, :, 0]
    col_basis = col_pairs[:, :, 1]
    test_rows = sketch[0, 0]
    middle = jnp.einsum("pkat,pkbt->pkab", row_coef, col_coef, precision=high)
    test_side = jnp.einsum("pat,pkbt->pkab", test_rows, col_basis, precision=high)
    folded = jnp.einsum("pkab,pkcb->pkac", test_side, middle, precision=high)
    sample_part = jnp.einsum("pkac,pkct->pat", folded, row_basis, precision=high)
    own_sketch = sent_and_summed(sample_part, "depth", 0)
    own_basis = orthonormal(own_sketch)
    bases = gathered_copies(own_basis, "depth", 0)
    inner_prod = jnp.einsum("pat,pkct->pkac", bases, row_basis, precision=high)
    turned = jnp.einsum("pkac,pkcb->pkab", inner_prod, middle, precision=high)
    project_part = jnp.einsum("pkab,pkbt->pat", turned, col_basis, precision=high)
    projected = sent_and_summed(project_part, "depth", 0)
    root_tile = math.sqrt(test_rows.shape[-1])
    return ((own_basis * root_tile)[None, None], (projected / root_tile)[None, None])


def solution(mesh):
    return jax.shard_map(
        shards,
        mesh=mesh,
        in_specs=(
            P("row", "depth", "col", None, None, None),
            P("row", "depth", None),
            P("col", "depth", "row", None, None, None),
            P("col", "depth", None),
            P("row", "col", None),
            P("row", "col", None, None, None),
        ),
        out_specs=(P("row", "col", "depth", None, None), P("row", "col", "depth", None, None)),
        check_vma=False,
    )
```

profile of v0, /device:TPU:1, one launch (start us, length us, event | category | flops | bytes accessed | tf_op | source)
XLA Modules:
  0.0 273.3 jit_solution(12288357249461976770)
XLA Ops:
  7.2 0.0 copy-start
  7.2 0.0 all-gather.7.cloned.1.call-start
  7.2 0.7 all-gather.7.cloned.1.call-update
  7.9 0.0 all-gather.5.cloned.1.call-start
  8.0 0.7 all-gather.5.cloned.1.call-update
  8.7 0.7 compare_select_fusion.1
  9.3 0.7 compare_and_fusion
  10.0 0.7 compare_select_fusion.3
  10.7 0.7 compare_and_fusion.1
  11.4 0.7 compare_and_fusion.3
  12.0 109.1 %all-gather.7.cloned.1.call-done = f32[16,1,1,2,64,1024]{5,4,3,2,1,0:T(8,128)} async-done(((f32[1,1,1,2,64,1024]{5,4,3,2,1,0:T(8,128)}), f32[16,1,1,2,64,1024]{5,4,3,2,1,0:T(8,128)}) %all-gather.7.cloned.1.call-update) | async-done | bytes 8388624 | tf_op jit(solution)/shard_map/all_gather | solution.py:52
  121.1 7.7 %gather_fusion.2 = f32[16,2,64,1024]{3,2,1,0:T(8,128)} fusion(f32[16,2,64,1024]{3,2,1,0:T(8,128)} %bitcast.97, s32[1024]{0:T(1024)S(1)} %pad_clamp_fusion.1), kind=kCustom, calls=%fused_computation.2.clone | custom fusion | bytes 16777280 | tf_op jit(solution)/shard_map/jit(_take)/gather | solution.py:54
  128.8 8.6 %broadcast_select_fusion = f32[16,2,64,1024]{3,2,1,0:T(8,128)} fusion(f32[16,2,64,1024]{3,2,1,0:T(8,128)} %gather_fusion.2, pred[16]{0:T(512)(128)(4,1)S(1)} %compare_and_fusion.1), kind=kLoop, calls=%fused_computation.4 | loop fusion | flops 2097152 | bytes 16777232 | tf_op jit(solution)/shard_map/jit(_take)/select_n | solution.py:54
  137.4 5.8 %gather_fusion.3 = f32[2,2,2,64,1024]{4,3,2,1,0:T(8,128)} fusion(f32[8,2,2,64,1024]{4,3,2,1,0:T(8,128)} %bitcast.94, s32[1024]{0:T(1024)S(1)} %pad_clamp_fusion), kind=kCustom, calls=%fused_computation.3.clone | custom fusion | bytes 4194312 | tf_op jit(solution)/shard_map/jit(_take)/gather | solution.py:59
  143.2 65.0 %all-gather.5.cloned.1.call-done = f32[16,1,1,2,64,1024]{5,4,3,2,1,0:T(8,128)} async-done(((f32[1,1,1,2,64,1024]{5,4,3,2,1,0:T(8,128)}), f32[16,1,1,2,64,1024]{5,4,3,2,1,0:T(8,128)}) %all-gather.5.cloned.1.call-update) | async-done | bytes 8388624 | tf_op jit(solution)/shard_map/all_gather | solution.py:53
  208.2 7.7 %gather_fusion = f32[16,2,64,1024]{3,2,1,0:T(8,128)} fusion(f32[16,2,64,1024]{3,2,1,0:T(8,128)} %bitcast.96, s32[1024]{0:T(1024)S(1)} %pad_clamp_fusion.3), kind=kCustom, calls=%fused_computation.clone | custom fusion | bytes 16777280 | tf_op jit(solution)/shard_map/jit(_take)/gather | solution.py:55
  215.8 8.6 %broadcast_select_fusion.1 = f32[16,2,64,1024]{3,2,1,0:T(8,128)} fusion(f32[16,2,64,1024]{3,2,1,0:T(8,128)} %gather_fusion, pred[16]{0:T(512)(128)(4,1)S(1)} %compare_and_fusion.3), kind=kLoop, calls=%fused_computation.5 | loop fusion | flops 2097152 | bytes 16777232 | tf_op jit(solution)/shard_map/jit(_take)/select_n | solution.py:55
  224.4 5.4 %gather_fusion.1 = f32[2,2,2,64,1024]{4,3,2,1,0:T(8,128)} fusion(f32[8,2,2,64,1024]{4,3,2,1,0:T(8,128)} %bitcast.95, s32[1024]{0:T(1024)S(1)} %pad_clamp_fusion.2), kind=kCustom, calls=%fused_computation.1.clone | custom fusion | bytes 4194312 | tf_op jit(solution)/shard_map/jit(_take)/gather | solution.py:60
  229.9 2.8 %copy_select_fusion = (f32[2,2,2,64,1024]{4,3,1,0,2:T(8,128)S(1)}, f32[2,2,2,64,1024]{4,3,1,0,2:T(8,128)S(1)}) fusion(f32[2,2,2,64,1024]{4,3,2,1,0:T(8,128)} %gather_fusion.3, pred[2]{0:T(512)(128)(4,1)S(1)} %get-tuple-element.4, f32[2,2,2,64,1024]{4,3,2,1,0:T(8,128)} %gather_fusion.1, pred[2]{0:T(512)(128)(4,1)S(1)} %get-tuple-element.8), kind=kLoop, calls=%fused_computation.6 | loop fusion | flops 1048576 | bytes 8388612 | tf_op jit(solution)/shard_map/jit(_take)/select_n | solution.py:59
  232.6 0.0 copy-start.1
  232.6 0.0 copy-done
  232.7 1.6 fusion.1
  234.3 1.1 fusion
  235.4 0.3 fusion.9
  235.7 0.0 copy-done.1
  235.7 0.7 convolution_bitcast_fusion.1
  236.4 4.6 %all_to_all.15 = f32[2,1,64,1024]{3,2,1,0:T(8,128)S(1)} all-to-all(f32[2,1,64,1024]{3,2,1,0:T(8,128)S(1)} %convolution_bitcast_fusion.1), channel_id=1, replica_groups=mesh['row'=16,'col'=16,'depth'=2] {'depth'}, dimensions={0} | all-to-all | bytes 1048576 | tf_op jit(solution)/shard_map/all_to_all | solution.py:19
  241.1 0.4 fusion.10
  241.4 0.1 copy.27
  241.5 5.8 %custom-call.7 = f32[1,64,64]{2,1,0:T(8,128)S(1)} custom-call(f32[1,64,64]{2,1,0:T(8,128)S(1)} %fusion.6), custom_call_target="Cholesky" | custom-call | tf_op jit(solution)/shard_map/jit(cholesky)/cholesky | solution.py:42
  247.4 0.6 compare_reduce_fusion
  248.1 0.7 fusion.5
  248.7 4.9 %custom-call.8 = f32[1,1,64,64]{2,3,1,0:T(8,128)S(1)} custom-call(f32[1,1,64,64]{3,2,1,0:T(8,128)S(1)} %fusion.5), custom_call_target="InvertDiagBlocksLowerTriangular" | custom-call | tf_op jit(solution)/shard_map/triangular_solve | solution.py:43
  253.6 0.0 copy-start.2
  253.6 0.4 fusion.7
  254.1 0.7 multiply_bitcast_fusion.1
  254.8 4.2 %all_to_all.16 = f32[2,1,64,1024]{3,2,1,0:T(8,128)S(1)} all-to-all(f32[2,1,64,1024]{3,2,1,0:T(8,128)S(1)} %broadcast_in_dim.33), channel_id=1, replica_groups=mesh['row'=16,'col'=16,'depth'=2] {'depth'}, dimensions={0} | all-to-all | bytes 1048576 | tf_op jit(solution)/shard_map/all_to_all | solution.py:31
  259.0 0.0 copy-done.2
  259.0 1.6 fusion.2
  260.6 0.3 fusion.11
  260.9 0.7 convolution_bitcast_fusion
  261.6 4.2 %all_to_all.17 = f32[2,1,64,1024]{3,2,1,0:T(8,128)S(1)} all-to-all(f32[2,1,64,1024]{3,2,1,0:T(8,128)S(1)} %convolution_bitcast_fusion), channel_id=1, replica_groups=mesh['row'=16,'col'=16,'depth'=2] {'depth'}, dimensions={0} | all-to-all | bytes 1048576 | tf_op jit(solution)/shard_map/all_to_all | solution.py:19
  265.8 0.7 multiply_bitcast_fusion
  (9 shorter events, 0.2 us)
Async XLA Ops:
  7.2 225.5 %copy-start = (f32[1,1,2,64,1024]{4,3,2,1,0:T(8,128)S(1)}, f32[1,1,2,64,1024]{4,3,2,1,0:T(8,128)}, u32[]{:S(2)}) copy-start(f32[1,1,2,64,1024]{4,3,2,1,0:T(8,128)} %param.15) | copy-start | bytes 1572868
  7.2 113.9 %all-gather.7.cloned.1.call-start = ((), (), s32[]{:S(2)}) async-start(), calls=%async_computation.4 | async-start | bytes 8912896 | tf_op jit(solution)/shard_map/all_gather | solution.py:52
  7.9 200.3 %all-gather.5.cloned.1.call-start = ((), (), s32[]{:S(2)}) async-start(), calls=%async_computation.3 | async-start | bytes 8912896 | tf_op jit(solution)/shard_map/all_gather | solution.py:53
  232.6 3.1 %copy-start.1 = (f32[2,2,2,64,1024]{4,3,1,0,2:T(8,128)}, f32[2,2,2,64,1024]{4,3,1,0,2:T(8,128)S(1)}, u32[]{:S(2)}) copy-start(f32[2,2,2,64,1024]{4,3,1,0,2:T(8,128)S(1)} %get-tuple-element.10) | copy-start | bytes 6291460
  253.6 5.4 %copy-start.2 = (f32[2,2,2,64,1024]{4,3,1,0,2:T(8,128)S(1)}, f32[2,2,2,64,1024]{4,3,1,0,2:T(8,128)}, u32[]{:S(2)}) copy-start(f32[2,2,2,64,1024]{4,3,1,0,2:T(8,128)} %copy-done.1) | copy-start | bytes 6291460
Sparse Core Ops, SparseCore 0:
  10.1 110.9 all-gather.6
  124.1 84.0 all-gather.4
where the time goes:
time: 274 us; the launch traced here: 273 us
  waiting for transfers between devices  175 us (64%)
  other arithmetic  36.9 us (13%)
  local copies, waits for them, and re-layouts  26.7 us (10%)
  between operations  14.2 us (5%)
  blocking collectives  12.9 us (5%)
  matrix products  7.07 us (3%)
    all_gather x1, waiting for transfers between devices, shards(): left_all = lax.all_gather(left_local, 'col', axis=0, tiled=True)  109 us
    all_gather x1, waiting for transfers between devices, shards(): up_all = lax.all_gather(up_local, 'row', axis=0, tiled=True)  65 us
    select_n x2, other arithmetic, shards(): left_pairs = jnp.take(left_all, left_table, axis=0)  9.27 us
    select_n x2, other arithmetic, shards(): up_pairs = jnp.take(up_all, up_table, axis=0)  9.26 us
    all_to_all x2, blocking collectives, sent_and_summed(): lax.all_to_all(split_up(shard, dim, devices), axis, 0, 0, tiled=True)  8.78 us
    gather x1, local copies, waits for them, and re-layouts, shards(): left_pairs = jnp.take(left_all, left_table, axis=0)  7.68 us
    gather x1, local copies, waits for them, and re-layouts, shards(): up_pairs = jnp.take(up_all, up_table, axis=0)  7.67 us
    another operation x3, other arithmetic, orthonormal(): factor_low = jnp.linalg.cholesky(gram_mat)  6.52 us
  transfers between devices with their start and end apart: 2, of which 2 were waited for; matrix products, arithmetic and copies ran while one was open for 9% of the time, Pallas kernels for 0%

commit v1 on v0

--- a/solution.py
+++ b/solution.py
@@ -7,6 +7,12 @@
 KD = 2
 RB = 8
 CB = 8
+
+
+def gather_from_all(x, axis, dim):
+    size = lax.axis_size(axis)
+    repeats = [size if d == dim else 1 for d in range(x.ndim)]
+    return lax.all_to_all(jnp.tile(x, repeats), axis, split_axis=dim, concat_axis=dim, tiled=True)
 
 
 def split_up(shard, dim, devices):
@@ -50,7 +56,7 @@
     left_table = left_home[0, 0]
     up_table = up_home[0, 0]
     left_all = lax.all_gather(left_local, "col", axis=0, tiled=True)
-    up_all = lax.all_gather(up_local, "row", axis=0, tiled=True)
+    up_all = gather_from_all(up_local, "row", 0)
     left_pairs = jnp.take(left_all, left_table, axis=0)
     up_pairs = jnp.take(up_all, up_table, axis=0)
     chosen = targets[0, 0]

time: 274 us -> 232 us (0.85)
  waiting for transfers between devices: 175 us -> 117 us
  starting transfers between devices: 0.08 us -> 7.79 us
  local copies, waits for them, and re-layouts: 26.7 us -> 31.7 us
  blocking collectives: 12.9 us -> 16.9 us
  other arithmetic: 36.9 us -> 33.6 us
    all_to_all x0 -> x1, waiting for transfers between devices: none -> 117 us  [gather_from_all(): lax.all_to_all(jnp.tile(x, repeats), axis, split_axis=dim, concat_axis=di...]
    all_gather x1, waiting for transfers between devices: 109 us -> 0.01 us  [shards(): left_all = lax.all_gather(left_local, 'col', axis=0, tiled=True)]
    all_gather x1 -> x0, waiting for transfers between devices: 65 us -> none  [shards(): up_all = lax.all_gather(up_local, 'row', axis=0, tiled=True)]
    all_to_all x0 -> x1, starting transfers between devices: none -> 7.76 us  [gather_from_all(): lax.all_to_all(jnp.tile(x, repeats), axis, split_axis=dim, concat_axis=di...]
    another operation x0 -> x1, local copies, waits for them, and re-layouts: none -> 5.32 us  [gather_from_all(): jnp.tile(x, repeats)]
    all_to_all x2, blocking collectives: 8.78 us -> 12.7 us  [sent_and_summed(): lax.all_to_all(split_up(shard, dim, devices), axis, 0, 0, tiled=True)]
  transfers between devices with their start and end apart: 2 -> 2, of which waited for: 2 -> 1; matrix products, arithmetic and copies ran while one was open for 9% -> 12% of each run, Pallas kernels for 0% -> 0%
where the time goes in v1:
time: 232 us; the launch traced here: 229 us
  waiting for transfers between devices  117 us (50%)
  other arithmetic  33.6 us (14%)
  local copies, waits for them, and re-layouts  31.7 us (14%)
  blocking collectives  16.9 us (7%)
  between operations  14.3 us (6%)
  starting transfers between devices  7.79 us (3%)
  matrix products  7.07 us (3%)
    all_to_all x1, waiting for transfers between devices, gather_from_all(): lax.all_to_all(jnp.tile(x, repeats), axis, split_axis=dim, concat_axis=di...  117 us
    all_to_all x2, blocking collectives, sent_and_summed(): lax.all_to_all(split_up(shard, dim, devices), axis, 0, 0, tiled=True)  12.7 us
    select_n x2, other arithmetic, shards(): left_pairs = jnp.take(left_all, left_table, axis=0)  8.61 us
    select_n x2, other arithmetic, shards(): up_pairs = jnp.take(up_all, up_table, axis=0)  8.61 us
    all_to_all x1, starting transfers between devices, gather_from_all(): lax.all_to_all(jnp.tile(x, repeats), axis, split_axis=dim, concat_axis=di...  7.76 us
    gather x1, local copies, waits for them, and re-layouts, shards(): left_pairs = jnp.take(left_all, left_table, axis=0)  7.68 us
    gather x1, local copies, waits for them, and re-layouts, shards(): up_pairs = jnp.take(up_all, up_table, axis=0)  7.67 us
    another operation x3, other arithmetic, orthonormal(): factor_low = jnp.linalg.cholesky(gram_mat)  6.52 us
  transfers between devices with their start and end apart: 2, of which 1 were waited for; matrix products, arithmetic and copies ran while one was open for 12% of the time, Pallas kernels for 0%

profile of v1, /device:TPU:1, one launch (start us, length us, event | category | flops | bytes accessed | tf_op | source)
XLA Modules:
  0.0 228.8 jit_solution(11892628957496668006)
XLA Ops:
  7.2 0.0 copy-start
  7.2 0.0 all-gather.3.cloned.1.call-start
  7.2 0.7 all-gather.3.cloned.1.call-update
  7.9 5.3 %tile.9 = f32[16,2,64,1024]{3,2,1,0:T(8,128)} broadcast(f32[2,64,1024]{2,1,0:T(8,128)} %bitcast.97), dimensions={1,2,3} | broadcast | bytes 8912896 | tf_op jit(solution)/shard_map/tile | solution.py:15
  13.2 0.0 copy-start.3
  13.2 0.0 copy-start.4
  13.2 0.0 copy-start.5
  13.2 7.8 %all-to-all-start = ((f32[16,2,64,1024]{3,2,1,0:T(8,128)}), f32[16,2,64,1024]{3,2,1,0:T(8,128)}, u32[]{:S(2)}, u32[]{:S(2)}) async-start(f32[16,2,64,1024]{3,2,1,0:T(8,128)} %tile.9), calls=%async_computation | async-start | bytes 16777216 | tf_op jit(solution)/shard_map/all_to_all | solution.py:15
  21.0 0.0 copy-done.3
  21.0 0.0 copy-done.4
  21.1 0.0 copy-done.5
  21.2 116.8 %all-to-all-done = f32[16,2,64,1024]{3,2,1,0:T(8,128)} async-done(((f32[16,2,64,1024]{3,2,1,0:T(8,128)}), f32[16,2,64,1024]{3,2,1,0:T(8,128)}, u32[]{:S(2)}, u32[]{:S(2)}) %all-to-all-start) | async-done | bytes 8388640 | tf_op jit(solution)/shard_map/all_to_all | solution.py:15
  138.0 7.7 %gather_fusion = f32[16,2,64,1024]{3,2,1,0:T(8,128)} fusion(f32[16,2,64,1024]{3,2,1,0:T(8,128)} %all-to-all-done, s32[1024]{0:T(1024)S(1)} %pad_clamp_fusion.3), kind=kCustom, calls=%fused_computation.clone | custom fusion | bytes 16777280 | tf_op jit(solution)/shard_map/jit(_take)/gather | solution.py:61
  145.6 8.6 %broadcast_select_fusion.1 = f32[16,2,64,1024]{3,2,1,0:T(8,128)} fusion(f32[16,2,64,1024]{3,2,1,0:T(8,128)} %gather_fusion, pred[16]{0:T(512)(128)(4,1)S(1)} %compare_and_fusion.3), kind=kLoop, calls=%fused_computation.5 | loop fusion | flops 2097152 | bytes 16777232 | tf_op jit(solution)/shard_map/jit(_take)/select_n | solution.py:61
  154.3 5.4 %gather_fusion.1 = f32[2,2,2,64,1024]{4,3,2,1,0:T(8,128)} fusion(f32[8,2,2,64,1024]{4,3,2,1,0:T(8,128)} %bitcast.94, s32[1024]{0:T(1024)S(1)} %pad_clamp_fusion.2), kind=kCustom, calls=%fused_computation.1.clone | custom fusion | bytes 4194312 | tf_op jit(solution)/shard_map/jit(_take)/gather | solution.py:66
  159.7 0.0 all-gather.3.cloned.1.call-done
  159.7 7.7 %gather_fusion.2 = f32[16,2,64,1024]{3,2,1,0:T(8,128)} fusion(f32[16,2,64,1024]{3,2,1,0:T(8,128)} %bitcast.96, s32[1024]{0:T(1024)S(1)} %pad_clamp_fusion.1), kind=kCustom, calls=%fused_computation.2.clone | custom fusion | bytes 16777280 | tf_op jit(solution)/shard_map/jit(_take)/gather | solution.py:60
  167.4 8.6 %broadcast_select_fusion = f32[16,2,64,1024]{3,2,1,0:T(8,128)} fusion(f32[16,2,64,1024]{3,2,1,0:T(8,128)} %gather_fusion.2, pred[16]{0:T(512)(128)(4,1)S(1)} %compare_and_fusion.1), kind=kLoop, calls=%fused_computation.4 | loop fusion | flops 2097152 | bytes 16777232 | tf_op jit(solution)/shard_map/jit(_take)/select_n | solution.py:60
  176.0 5.4 %gather_fusion.3 = f32[2,2,2,64,1024]{4,3,2,1,0:T(8,128)} fusion(f32[8,2,2,64,1024]{4,3,2,1,0:T(8,128)} %bitcast.95, s32[1024]{0:T(1024)S(1)} %pad_clamp_fusion), kind=kCustom, calls=%fused_computation.3.clone | custom fusion | bytes 4194312 | tf_op jit(solution)/shard_map/jit(_take)/gather | solution.py:65
  181.4 2.8 %copy_select_fusion = (f32[2,2,2,64,1024]{4,3,1,0,2:T(8,128)S(1)}, f32[2,2,2,64,1024]{4,3,1,0,2:T(8,128)S(1)}) fusion(f32[2,2,2,64,1024]{4,3,2,1,0:T(8,128)} %gather_fusion.3, pred[2]{0:T(512)(128)(4,1)S(1)} %get-tuple-element.4, f32[2,2,2,64,1024]{4,3,2,1,0:T(8,128)} %gather_fusion.1, pred[2]{0:T(512)(128)(4,1)S(1)} %get-tuple-element.8), kind=kLoop, calls=%fused_computation.6 | loop fusion | flops 1048576 | bytes 8388612 | tf_op jit(solution)/shard_map/jit(_take)/select_n | solution.py:65
  184.1 0.0 copy-start.1
  184.2 1.1 fusion
  185.3 0.0 copy-done
  185.3 1.6 fusion.1
  186.9 0.3 fusion.9
  187.2 0.0 copy-done.1
  187.2 0.7 convolution_bitcast_fusion.1
  187.9 8.6 %all_to_all.20 = f32[2,1,64,1024]{3,2,1,0:T(8,128)S(1)} all-to-all(f32[2,1,64,1024]{3,2,1,0:T(8,128)S(1)} %convolution_bitcast_fusion.1), channel_id=1, replica_groups=mesh['row'=16,'col'=16,'depth'=2] {'depth'}, dimensions={0} | all-to-all | bytes 1048576 | tf_op jit(solution)/shard_map/all_to_all | solution.py:25
  196.5 0.4 fusion.10
  196.9 0.1 copy.27
  197.0 5.8 %custom-call.7 = f32[1,64,64]{2,1,0:T(8,128)S(1)} custom-call(f32[1,64,64]{2,1,0:T(8,128)S(1)} %fusion.6), custom_call_target="Cholesky" | custom-call | tf_op jit(solution)/shard_map/jit(cholesky)/cholesky | solution.py:48
  202.9 0.6 compare_reduce_fusion
  203.5 0.7 fusion.5
  204.2 4.9 %custom-call.8 = f32[1,1,64,64]{2,3,1,0:T(8,128)S(1)} custom-call(f32[1,1,64,64]{3,2,1,0:T(8,128)S(1)} %fusion.5), custom_call_target="InvertDiagBlocksLowerTriangular" | custom-call | tf_op jit(solution)/shard_map/triangular_solve | solution.py:49
  209.1 0.0 copy-start.2
  209.1 0.4 fusion.7
  209.5 0.7 multiply_bitcast_fusion.1
  210.3 4.2 %all_to_all.21 = f32[2,1,64,1024]{3,2,1,0:T(8,128)S(1)} all-to-all(f32[2,1,64,1024]{3,2,1,0:T(8,128)S(1)} %broadcast_in_dim.33), channel_id=1, replica_groups=mesh['row'=16,'col'=16,'depth'=2] {'depth'}, dimensions={0} | all-to-all | bytes 1048576 | tf_op jit(solution)/shard_map/all_to_all | solution.py:37
  214.4 0.0 copy-done.2
  214.4 1.6 fusion.2
  216.1 0.3 fusion.11
  216.3 0.7 convolution_bitcast_fusion
  217.0 4.2 %all_to_all.22 = f32[2,1,64,1024]{3,2,1,0:T(8,128)S(1)} all-to-all(f32[2,1,64,1024]{3,2,1,0:T(8,128)S(1)} %convolution_bitcast_fusion), channel_id=1, replica_groups=mesh['row'=16,'col'=16,'depth'=2] {'depth'}, dimensions={0} | all-to-all | bytes 1048576 | tf_op jit(solution)/shard_map/all_to_all | solution.py:25
  221.2 0.7 multiply_bitcast_fusion
  (14 shorter events, 0.2 us)
Async XLA Ops:
  7.2 178.1 %copy-start = (f32[1,1,2,64,1024]{4,3,2,1,0:T(8,128)S(1)}, f32[1,1,2,64,1024]{4,3,2,1,0:T(8,128)}, u32[]{:S(2)}) copy-start(f32[1,1,2,64,1024]{4,3,2,1,0:T(8,128)} %param.15) | copy-start | bytes 1572868
  7.2 152.5 %all-gather.3.cloned.1.call-start = ((), (), s32[]{:S(2)}) async-start(), calls=%async_computation.4 | async-start | bytes 8912896 | tf_op jit(solution)/shard_map/all_gather | solution.py:58
  13.2 7.8 %copy-start.3 = (s32[1,1,2]{2,1,0:T(1,128)S(1)}, s32[1,1,2]{2,1,0:T(1,128)}, u32[]{:S(2)}) copy-start(s32[1,1,2]{2,1,0:T(1,128)} %param.14) | copy-start | bytes 28
  13.2 7.8 %copy-start.4 = (s32[1,1,16]{2,1,0:T(1,128)S(1)}, s32[1,1,16]{2,1,0:T(1,128)}, u32[]{:S(2)}) copy-start(s32[1,1,16]{2,1,0:T(1,128)} %param.13) | copy-start | bytes 196
  13.2 7.9 %copy-start.5 = (s32[1,1,16]{2,1,0:T(1,128)S(1)}, s32[1,1,16]{2,1,0:T(1,128)}, u32[]{:S(2)}) copy-start(s32[1,1,16]{2,1,0:T(1,128)} %param.11) | copy-start | bytes 196
  13.2 124.7 %all-to-all-start = ((f32[16,2,64,1024]{3,2,1,0:T(8,128)}), f32[16,2,64,1024]{3,2,1,0:T(8,128)}, u32[]{:S(2)}, u32[]{:S(2)}) async-start(f32[16,2,64,1024]{3,2,1,0:T(8,128)} %tile.9), calls=%async_computation | async-start | bytes 16777216 | tf_op jit(solution)/shard_map/all_to_all | solution.py:15
  184.1 3.1 %copy-start.1 = (f32[2,2,2,64,1024]{4,3,1,0,2:T(8,128)}, f32[2,2,2,64,1024]{4,3,1,0,2:T(8,128)S(1)}, u32[]{:S(2)}) copy-start(f32[2,2,2,64,1024]{4,3,1,0,2:T(8,128)S(1)} %get-tuple-element.10) | copy-start | bytes 6291460
  209.1 5.4 %copy-start.2 = (f32[2,2,2,64,1024]{4,3,1,0,2:T(8,128)S(1)}, f32[2,2,2,64,1024]{4,3,1,0,2:T(8,128)}, u32[]{:S(2)}) copy-start(f32[2,2,2,64,1024]{4,3,1,0,2:T(8,128)} %copy-done.1) | copy-start | bytes 6291460
Sparse Core Ops, SparseCore 0:
  10.1 110.9 all-gather.2
